TPU v7x, 32 devices: a whole 2x2x4 slice. The times are simulated.
32 devices in a mesh: seq: 8 (over z, y), head: 4 (over x, core).
Axes of the slice: x: 2, y: 2, z: 4, core: 2. Of those that a mesh axis runs over, the one named last changes fastest.
Arguments:
- layer_input: bfloat16 [4096, 768], P('seq', 'head'), may hold values from -6 to 6
- ln1_gain: float32 [768], replicated, may hold values from 0.5 to 1.5
- ln1_bias: float32 [768], replicated, may hold values from -3 to 3
- w_query: bfloat16 [768, 768], P(None, 'head'), may hold values from -0.21875 to 0.21875
- b_query: float32 [768], P('head'), may hold values from -3 to 3
- w_key: bfloat16 [768, 768], P(None, 'head'), may hold values from -0.3125 to 0.3125
- w_value: bfloat16 [768, 768], P(None, 'head'), may hold values from -0.21875 to 0.21875
- b_value: float32 [768], P('head'), may hold values from -1.2 to 1.2
- sub_gain: float32 [768], P('head'), may hold values from 0.5 to 1.5
- sub_bias: float32 [768], P('head'), may hold values from -3 to 3
- w_out: bfloat16 [768, 768], P('head'), may hold values from -0.21875 to 0.21875
- b_out: float32 [768], replicated, may hold values from -3 to 3
- ln2_gain: float32 [768], replicated, may hold values from 0.5 to 1.5
- ln2_bias: float32 [768], replicated, may hold values from -3 to 3
- w_up: bfloat16 [768, 3072], P(None, 'head'), may hold values from -0.21875 to 0.21875
- b_up: float32 [3072], P('head'), may hold values from -3 to 3
- w_down: bfloat16 [3072, 768], P('head'), may hold values from -0.109375 to 0.109375
- b_down: float32 [768], replicated, may hold values from -3 to 3
- cotangent: bfloat16 [4096, 768], P('seq', 'head'), may hold values from -6 to 6
- row_lengths: int32 [6], replicated, may hold values from 1 to 3072, 4096 in all
Outputs:
- layer_output: bfloat16 [4096, 768], P('seq', 'head')
- grad_input: float32 [4096, 768], P('seq', 'head')
- grad_ln1_gain: float32 [768], replicated
- grad_ln1_bias: float32 [768], replicated
- grad_w_query: float32 [768, 768], P(None, 'head')
- grad_b_query: float32 [768], P('head')
- grad_w_key: float32 [768, 768], P(None, 'head')
- grad_w_value: float32 [768, 768], P(None, 'head')
- grad_b_value: float32 [768], P('head')
- grad_sub_gain: float32 [768], P('head')
- grad_sub_bias: float32 [768], P('head')
- grad_w_out: float32 [768, 768], P('head')
- grad_b_out: float32 [768], replicated
- grad_ln2_gain: float32 [768], replicated
- grad_ln2_bias: float32 [768], replicated
- grad_w_up: float32 [768, 3072], P(None, 'head')
- grad_b_up: float32 [3072], P('head')
- grad_w_down: float32 [3072, 768], P('head')
- grad_b_down: float32 [768], replicated
Inputs may be any that keep to these rules, and one draw needn't show every extreme that they name: `row_lengths`: the 6 row lengths sum to 4096, and the longest is exactly 3072.
All inputs are finite; a program needn't handle non-finite values.
Results may differ from a plain program's by a relative error of at most 0.018.
Values may be sent and summed in bfloat16 or wider, within the bound.
No kernel may reach another device: no remote copies, remote signals or barrier semaphores. Data moves between devices by JAX's collectives and lax.ppermute only.
A program may use at most 256 MiB of HBM per device.

v0:
```python
import math
import jax
import jax.numpy as jnp
from jax import lax
from jax.sharding import PartitionSpec as P

HEAD_DIM = 64
SEG = 2048
eps = 1e-05
segment_scales = (1, 2, 4, 8, 16)
dilation_steps = (1, 2, 4, 6, 12)


def layer_norm(inputs, norm_gain, norm_bias):
    center = inputs - jnp.mean(inputs, axis=-1, keepdims=True)
    spread = jnp.mean(center * center, axis=-1, keepdims=True)
    return center * lax.rsqrt(spread + eps) * norm_gain + norm_bias


def token_places(positions, lengths):
    row_ends = jnp.cumsum(lengths)
    starts = row_ends - lengths
    row_of = jnp.sum((positions[:, None] >= row_ends[None, :]).astype(jnp.int32), axis=1)
    onehot = (row_of[:, None] == jnp.arange(lengths.shape[0], dtype=jnp.int32)[None, :]).astype(
        jnp.int32
    )
    row_place = positions - jnp.sum(onehot * starts[None, :], axis=1)
    return (row_of, row_place)


def pattern_count(head_ids, query_row, query_place, key_row, key_place):
    allowed = (query_row[:, None] == key_row[None, :]) & (
        key_place[None, :] <= query_place[:, None]
    )
    counted = jnp.zeros((head_ids.shape[0], query_row.shape[0], key_row.shape[0]), jnp.float32)
    for scale_factor, step_size in zip(segment_scales, dilation_steps):
        seg_width = SEG * scale_factor
        same_seg = allowed & (query_place[:, None] // seg_width == key_place[None, :] // seg_width)
        offset = head_ids % step_size
        query_on = (query_place % seg_width % step_size)[None, :] == offset[:, None]
        key_on = (key_place % seg_width % step_size)[None, :] == offset[:, None]
        counted = counted + (same_seg[None] & query_on[:, :, None] & key_on[:, None, :]).astype(
            jnp.float32
        )
    return counted


def fold_keys(running, pieces, queries, head_ids, query_row, query_place, lengths, score_scale):
    key_rows, values = pieces
    piece_rows = key_rows.shape[0]
    block_rows = math.gcd(piece_rows, 2048)
    local_heads = queries.shape[0]
    key_blocks = key_rows.reshape(piece_rows // block_rows, block_rows, local_heads, -1)
    value_blocks = values.reshape(piece_rows // block_rows, block_rows, local_heads, -1)
    offsets = jnp.arange(piece_rows // block_rows, dtype=jnp.int32) * block_rows

    def advance(status, element):
        highest, totals, running_sum = status
        key_blk, value_blk, block_first = element
        key_row, key_place = token_places(
            block_first + jnp.arange(block_rows, dtype=jnp.int32), lengths
        )
        counted = pattern_count(head_ids, query_row, query_place, key_row, key_place)
        scores = (
            jnp.einsum("hqd,khd->hqk", queries, key_blk, preferred_element_type=jnp.float32)
            * score_scale
        )
        masked = jnp.where(counted > 0, scores, -1e30)
        new_high = jnp.maximum(highest, jnp.max(masked, axis=-1))
        weights = counted * jnp.exp(masked - new_high[..., None])
        factor = jnp.exp(highest - new_high)
        totals = totals * factor + jnp.sum(weights, axis=-1)
        running_sum = running_sum * factor[..., None] + jnp.einsum(
            "hqk,khd->hqd",
            weights.astype(jnp.bfloat16),
            value_blk,
            preferred_element_type=jnp.float32,
        )
        return ((new_high, totals, running_sum), None)

    running, unused = lax.scan(advance, running, (key_blocks, value_blocks, offsets))
    return running


def shards(
    layer_input,
    ln1_gain,
    ln1_bias,
    w_query,
    b_query,
    w_key,
    w_value,
    b_value,
    sub_gain,
    sub_bias,
    w_out,
    b_out,
    ln2_gain,
    ln2_bias,
    w_up,
    b_up,
    w_down,
    b_down,
    cotangent,
    row_lengths,
):
    rows_local = layer_input.shape[0]
    slice_width = layer_input.shape[1]
    head_share = w_query.shape[1]
    local_heads = head_share // HEAD_DIM
    head_pos = lax.axis_index("head")
    seq_pos = lax.axis_index("seq")
    full_width = head_share * lax.axis_size("head")
    score_scale = HEAD_DIM ** (-0.5)
    head_ids = head_pos * local_heads + jnp.arange(local_heads, dtype=jnp.int32)
    own_index = seq_pos * rows_local + jnp.arange(rows_local, dtype=jnp.int32)
    query_row, query_place = token_places(own_index, row_lengths)
    input_whole = lax.all_gather(layer_input, "head", axis=1, tiled=True).astype(jnp.float32)
    normed = layer_norm(input_whole, ln1_gain, ln1_bias).astype(jnp.bfloat16)
    queries = (jnp.dot(normed, w_query, preferred_element_type=jnp.float32) + b_query).astype(
        jnp.bfloat16
    )
    key_rows = jnp.dot(normed, w_key, preferred_element_type=jnp.float32).astype(jnp.bfloat16)
    values = (jnp.dot(normed, w_value, preferred_element_type=jnp.float32) + b_value).astype(
        jnp.bfloat16
    )
    query_heads = queries.reshape(rows_local, local_heads, HEAD_DIM).transpose(1, 0, 2)
    start_state = (
        jnp.full((local_heads, rows_local), -1e30, jnp.float32),
        jnp.zeros((local_heads, rows_local), jnp.float32),
        jnp.zeros((local_heads, rows_local, HEAD_DIM), jnp.float32),
    )
    highest, totals, running_sum = fold_keys(
        start_state,
        (
            lax.all_gather(key_rows, "seq", axis=0, tiled=True),
            lax.all_gather(values, "seq", axis=0, tiled=True),
        ),
        query_heads,
        head_ids,
        query_row,
        query_place,
        row_lengths,
        score_scale,
    )
    attended = running_sum / totals[..., None]
    log_total = highest + jnp.log(totals)
    mixed_heads = attended.transpose(1, 0, 2).reshape(rows_local, head_share)
    row_sum, row_square = lax.psum(
        (jnp.sum(mixed_heads, axis=1), jnp.sum(mixed_heads * mixed_heads, axis=1)), "head"
    )
    mean_value = row_sum / full_width
    inv_std = lax.rsqrt(row_square / full_width - mean_value * mean_value + eps)
    centered = (mixed_heads - mean_value[:, None]) * inv_std[:, None]
    sub_out = (centered * sub_gain + sub_bias).astype(jnp.bfloat16)
    projected = lax.psum_scatter(
        jnp.dot(sub_out, w_out, preferred_element_type=jnp.float32).astype(jnp.bfloat16),
        "head",
        scatter_dimension=1,
        tiled=True,
    ).astype(jnp.float32)
    out_bias_share = lax.dynamic_slice_in_dim(b_out, head_pos * slice_width, slice_width, 0)
    middle = layer_input.astype(jnp.float32) + (projected + out_bias_share)
    middle_whole = lax.all_gather(middle.astype(jnp.bfloat16), "head", axis=1, tiled=True).astype(
        middle.dtype
    )
    normed_mid = layer_norm(middle_whole, ln2_gain, ln2_bias).astype(jnp.bfloat16)
    inner_act = jnp.dot(normed_mid, w_up, preferred_element_type=jnp.float32) + b_up
    active = jax.nn.gelu(inner_act, approximate=False).astype(jnp.bfloat16)
    ffn_out = lax.psum_scatter(
        jnp.dot(active, w_down, preferred_element_type=jnp.float32).astype(jnp.bfloat16),
        "head",
        scatter_dimension=1,
        tiled=True,
    ).astype(jnp.float32)
    down_bias_share = lax.dynamic_slice_in_dim(b_down, head_pos * slice_width, slice_width, 0)
    layer_output = (middle + (ffn_out + down_bias_share)).astype(jnp.bfloat16)
    grad_whole = lax.all_gather(cotangent, "head", axis=1, tiled=True)
    grad_float = grad_whole.astype(jnp.float32)
    grad_w_down = jnp.dot(active.T, grad_whole, preferred_element_type=jnp.float32)
    grad_b_down = jnp.sum(grad_float, axis=0)
    grad_active = jnp.dot(grad_whole, w_down.T, preferred_element_type=jnp.float32)
    unused, gelu_back = jax.vjp(lambda inputs: jax.nn.gelu(inputs, approximate=False), inner_act)
    grad_inner = gelu_back(grad_active)[0].astype(jnp.bfloat16)
    grad_w_up = jnp.dot(normed_mid.T, grad_inner, preferred_element_type=jnp.float32)
    grad_b_up = jnp.sum(grad_inner.astype(jnp.float32), axis=0)
    grad_norm_mid = lax.psum(
        jnp.dot(grad_inner, w_up.T, preferred_element_type=jnp.float32).astype(jnp.bfloat16), "head"
    ).astype(jnp.float32)
    unused, mid_back = jax.vjp(layer_norm, middle_whole, ln2_gain, ln2_bias)
    grad_mid_norm, grad_ln2_gain, grad_ln2_bias = mid_back(grad_norm_mid)
    grad_middle = grad_float + grad_mid_norm
    grad_branch = grad_middle.astype(jnp.bfloat16)
    grad_b_out = jnp.sum(grad_branch.astype(jnp.float32), axis=0)
    grad_w_out = jnp.dot(sub_out.T, grad_branch, preferred_element_type=jnp.float32)
    grad_sub = jnp.dot(grad_branch, w_out.T, preferred_element_type=jnp.float32)
    grad_sub_gain = jnp.sum(grad_sub * centered, axis=0)
    grad_sub_bias = jnp.sum(grad_sub, axis=0)
    grad_hat = grad_sub * sub_gain
    hat_sum, hat_cross = lax.psum(
        (jnp.sum(grad_hat, axis=1), jnp.sum(grad_hat * centered, axis=1)), "head"
    )
    grad_mixed = inv_std[:, None] * (
        grad_hat - hat_sum[:, None] / full_width - centered * hat_cross[:, None] / full_width
    )
    grad_heads = (
        grad_mixed.reshape(rows_local, local_heads, HEAD_DIM)
        .transpose(1, 0, 2)
        .astype(jnp.bfloat16)
    )
    dot_term = jnp.sum(grad_heads.astype(jnp.float32) * attended, axis=-1)
    key_all, value_all = (
        lax.all_gather(key_rows, "seq", axis=0, tiled=True),
        lax.all_gather(values, "seq", axis=0, tiled=True),
    )
    total_rows = key_all.shape[0]
    block_rows = math.gcd(total_rows, 2048)
    key_blocks = key_all.reshape(total_rows // block_rows, block_rows, local_heads, HEAD_DIM)
    value_blocks = value_all.reshape(total_rows // block_rows, block_rows, local_heads, HEAD_DIM)
    offsets = jnp.arange(total_rows // block_rows, dtype=jnp.int32) * block_rows

    def score_parts(
        query_blk, grad_blk, log_blk, dot_blk, q_row, q_place, key_blk, value_blk, k_row, k_place
    ):
        counted = pattern_count(head_ids, q_row, q_place, k_row, k_place)
        scores = (
            jnp.einsum("hqd,khd->hqk", query_blk, key_blk, preferred_element_type=jnp.float32)
            * score_scale
        )
        masked = jnp.where(counted > 0, scores, -1e30)
        weights_norm = counted * jnp.exp(masked - log_blk[..., None])
        grad_probs = jnp.einsum(
            "hqd,khd->hqk", grad_blk, value_blk, preferred_element_type=jnp.float32
        )
        grad_scores = (weights_norm * (grad_probs - dot_blk[..., None])).astype(jnp.bfloat16)
        return (weights_norm, grad_scores)

    def back_step(grad_query_sum, element):
        key_blk, value_blk, block_first = element
        key_row, key_place = token_places(
            block_first + jnp.arange(block_rows, dtype=jnp.int32), row_lengths
        )
        weights_norm, grad_scores = score_parts(
            query_heads,
            grad_heads,
            log_total,
            dot_term,
            query_row,
            query_place,
            key_blk,
            value_blk,
            key_row,
            key_place,
        )
        grad_query_sum = grad_query_sum + jnp.einsum(
            "hqk,khd->hqd", grad_scores, key_blk, preferred_element_type=jnp.float32
        )
        grad_value = jnp.einsum(
            "hqk,hqd->khd",
            weights_norm.astype(jnp.bfloat16),
            grad_heads,
            preferred_element_type=jnp.float32,
        )
        grad_key = jnp.einsum(
            "hqk,hqd->khd", grad_scores, query_heads, preferred_element_type=jnp.float32
        )
        key_terms = jnp.concatenate(
            [grad_key.reshape(block_rows, -1) * score_scale, grad_value.reshape(block_rows, -1)],
            axis=1,
        )
        return (grad_query_sum, key_terms)

    query_zero = jnp.zeros((local_heads, rows_local, HEAD_DIM), jnp.float32)
    grad_query_sum, key_terms = lax.scan(back_step, query_zero, (key_blocks, value_blocks, offsets))
    key_terms = key_terms.reshape(total_rows, 2 * head_share)
    kv_grads = lax.psum_scatter(key_terms, "seq", scatter_dimension=0, tiled=True)
    grad_keys = kv_grads[:, :head_share].astype(jnp.bfloat16)
    grad_values = kv_grads[:, head_share:].astype(jnp.bfloat16)
    grad_queries = (grad_query_sum * score_scale).transpose(1, 0, 2).reshape(rows_local, head_share)
    grad_queries = grad_queries.astype(jnp.bfloat16)
    grad_w_query = jnp.dot(normed.T, grad_queries, preferred_element_type=jnp.float32)
    grad_b_query = jnp.sum(grad_queries.astype(jnp.float32), axis=0)
    grad_w_key = jnp.dot(normed.T, grad_keys, preferred_element_type=jnp.float32)
    grad_w_value = jnp.dot(normed.T, grad_values, preferred_element_type=jnp.float32)
    grad_b_value = jnp.sum(grad_values.astype(jnp.float32), axis=0)
    grad_normed = (
        jnp.dot(grad_queries, w_query.T, preferred_element_type=jnp.float32)
        + jnp.dot(grad_keys, w_key.T, preferred_element_type=jnp.float32)
        + jnp.dot(grad_values, w_value.T, preferred_element_type=jnp.float32)
    )
    grad_normed = lax.psum(grad_normed.astype(jnp.bfloat16), "head").astype(jnp.float32)
    unused, input_back = jax.vjp(layer_norm, input_whole, ln1_gain, ln1_bias)
    grad_in_norm, grad_ln1_gain, grad_ln1_bias = input_back(grad_normed)
    grad_input_whole = grad_middle + grad_in_norm
    grad_input = lax.dynamic_slice_in_dim(grad_input_whole, head_pos * slice_width, slice_width, 1)
    summed = lax.psum(
        (
            grad_ln1_gain,
            grad_ln1_bias,
            grad_w_query,
            grad_b_query,
            grad_w_key,
            grad_w_value,
            grad_b_value,
            grad_sub_gain,
            grad_sub_bias,
            grad_w_out,
            grad_b_out,
            grad_ln2_gain,
            grad_ln2_bias,
            grad_w_up,
            grad_b_up,
            grad_w_down,
            grad_b_down,
        ),
        "seq",
    )
    return (layer_output, grad_input) + tuple(summed)


def solution(mesh):
    in_specs = (
        P("seq", "head"),
        P(),
        P(),
        P(None, "head"),
        P("head"),
        P(None, "head"),
        P(None, "head"),
        P("head"),
        P("head"),
        P("head"),
        P("head", None),
        P(),
        P(),
        P(),
        P(None, "head"),
        P("head"),
        P("head", None),
        P(),
        P("seq", "head"),
        P(),
    )
    out_specs = (
        P("seq", "head"),
        P("seq", "head"),
        P(),
        P(),
        P(None, "head"),
        P("head"),
        P(None, "head"),
        P(None, "head"),
        P("head"),
        P("head"),
        P("head"),
        P("head", None),
        P(),
        P(),
        P(),
        P(None, "head"),
        P("head"),
        P("head", None),
        P(),
    )
    return jax.shard_map(shards, mesh=mesh, in_specs=in_specs, out_specs=out_specs, check_vma=False)
```

profile of v0, /device:TPU:0, one launch (start us, length us, event | category | flops | bytes accessed | tf_op | source)
XLA Modules:
  0.0 842.9 jit_solution(17732856070422200237)
XLA Ops:
  7.3 10.4 %all_gather.17 = bf16[512,768]{0,1:T(8,128)(2,1)S(1)} all-gather(bf16[512,192]{0,1:T(8,128)(2,1)} %param.24), channel_id=1, replica_groups=mesh['seq'=8,'head'=4] {'head'}, dimensions={1}, use_global_device_ids=true | all-gather | bytes 983040 | tf_op jit(solution)/shard_map/all_gather | solution.py:118
  22.7 43.9 %all-gather.3.cloned.1.call-done = bf16[4096,192]{0,1:T(8,128)(2,1)} async-done(((bf16[512,192]{0,1:T(8,128)(2,1)}), bf16[4096,192]{0,1:T(8,128)(2,1)}) %all-gather.3.cloned.1.call-update) | async-done | bytes 1572880 | tf_op jit(solution)/shard_map/all_gather | solution.py:136
  66.6 2.9 reshape.2798
  71.2 41.5 %all-gather.5.cloned.1.call-done = bf16[4096,192]{0,1:T(8,128)(2,1)} async-done(((bf16[512,192]{0,1:T(8,128)(2,1)}), bf16[4096,192]{0,1:T(8,128)(2,1)}) %all-gather.5.cloned.1.call-update) | async-done | bytes 1572880 | tf_op jit(solution)/shard_map/all_gather | solution.py:137
  112.8 2.9 reshape.2800
  117.4 77.7 %while.42 = (s32[]{:T(128)}, f32[3,512]{1,0:T(4,128)S(1)}, f32[3,512]{1,0:T(4,128)}, f32[3,512,64]{1,2,0:T(8,128)}, s32[512]{0:T(512)S(1)}, /*index=5*/s32[2]{0:...) while((s32[]{:T(128)}, f32[3,512]{1,0:T(4,128)S(1)}, ...), condition=%wide.region_10.11_spmd.clone.clone.clone, body=%wide.region_5.10_spmd.clone.clone.clone.sunk | while | flops 955956864 | bytes 106965376 | solution.py:81
  120.3 4.1 compare_and_fusion.12
  125.2 12.1 %fusion.202 = (f32[3,512]{1,0:T(4,128)S(1)}, f32[3,2048,512]{2,1,0:T(8,128)}) fusion(f32[512,2048]{0,1:T(8,128)S(1)} %get-tuple-element.1711, pred[3,2048]{1,0:T(4,128)(4,1)S(1)} %broadcast_compare_fusion.38, pred[3,512]{1,0:T(4,128)(4,1)S(1)} %broadcast_compare_fusion.39, pred[512,2048]{0,1:T(8,128)(4,1)S(1)} %get-tuple-element.1716, ...), kind=kOutput, calls=%fused_computation.7.clone.1 | convolution fusion | flops 465566208 | bytes 22001668 | tf_op jit(solution)/shard_map/while/body/eval_jaxpr/hqd,khd->hqk/dot_general | solution.py:65
  137.4 16.7 %fusion.203 = (f32[3,512]{1,0:T(4,128)S(1)}, bf16[3,512,2048]{1,2,0:T(8,128)(2,1)S(1)}) fusion(f32[3,512]{1,0:T(4,128)S(1)} %select_maximum_fusion.2, f32[3,2048,512]{2,1,0:T(8,128)} %get-tuple-element.1730, pred[3,2048]{1,0:T(4,128)(4,1)S(1)} %broadcast_compare_fusion.38, pred[3,512]{1,0:T(4,128)(4,1)S(1)} %broadcast_compare_fusion.39, ...), kind=kLoop, calls=%fused_computation.388.clone.1 | loop fusion | flops 72350208 | bytes 27305984 | tf_op jit(solution)/shard_map/while/body/eval_jaxpr/reduce_sum | solution.py:72
  159.2 4.1 compare_and_fusion.12
  164.1 12.1 %fusion.202 = (f32[3,512]{1,0:T(4,128)S(1)}, f32[3,2048,512]{2,1,0:T(8,128)}) fusion(f32[512,2048]{0,1:T(8,128)S(1)} %get-tuple-element.1711, pred[3,2048]{1,0:T(4,128)(4,1)S(1)} %broadcast_compare_fusion.38, pred[3,512]{1,0:T(4,128)(4,1)S(1)} %broadcast_compare_fusion.39, pred[512,2048]{0,1:T(8,128)(4,1)S(1)} %get-tuple-element.1716, ...), kind=kOutput, calls=%fused_computation.7.clone.1 | convolution fusion | flops 465566208 | bytes 22001668 | tf_op jit(solution)/shard_map/while/body/eval_jaxpr/hqd,khd->hqk/dot_general | solution.py:65
  176.3 16.7 %fusion.203 = (f32[3,512]{1,0:T(4,128)S(1)}, bf16[3,512,2048]{1,2,0:T(8,128)(2,1)S(1)}) fusion(f32[3,512]{1,0:T(4,128)S(1)} %select_maximum_fusion.2, f32[3,2048,512]{2,1,0:T(8,128)} %get-tuple-element.1730, pred[3,2048]{1,0:T(4,128)(4,1)S(1)} %broadcast_compare_fusion.38, pred[3,512]{1,0:T(4,128)(4,1)S(1)} %broadcast_compare_fusion.39, ...), kind=kLoop, calls=%fused_computation.388.clone.1 | loop fusion | flops 72350208 | bytes 27305984 | tf_op jit(solution)/shard_map/while/body/eval_jaxpr/reduce_sum | solution.py:72
  196.4 6.0 all-reduce.3
  204.9 8.7 %all_gather.21 = bf16[512,768]{0,1:T(8,128)(2,1)S(1)} all-gather(bf16[512,192]{0,1:T(8,128)(2,1)} %param.42), channel_id=1, replica_groups=mesh['seq'=8,'head'=4] {'head'}, dimensions={1}, use_global_device_ids=true | all-gather | bytes 983040 | tf_op jit(solution)/shard_map/all_gather | solution.py:178
  213.6 11.9 %reduce-scatter.4.cloned.1.call-done = bf16[512,192]{0,1:T(8,128)(2,1)} async-done(((bf16[512,768]{0,1:T(8,128)(2,1)}), bf16[512,192]{0,1:T(8,128)(2,1)}) %reduce-scatter.4.cloned.1.call-update) | async-done | bytes 196624 | tf_op jit(solution)/shard_map/reduce_scatter | solution.py:156
  226.7 8.7 %all_gather.20 = bf16[512,768]{0,1:T(8,128)(2,1)S(1)} all-gather(bf16[512,192]{0,1:T(8,128)(2,1)S(1)} %fusion.114), channel_id=1, replica_groups=mesh['seq'=8,'head'=4] {'head'}, dimensions={1}, use_global_device_ids=true | all-gather | bytes 983040 | tf_op jit(solution)/shard_map/all_gather | solution.py:164
  237.0 5.8 convert_reduce_fusion.7
  246.1 34.5 %all-reduce.8.cloned.1.call-done = bf16[512,768]{0,1:T(8,128)(2,1)} async-done(((bf16[512,768]{0,1:T(8,128)(2,1)}), bf16[512,768]{0,1:T(8,128)(2,1)}) %all-reduce.8.cloned.1.call-update) | async-done | bytes 786448 | tf_op jit(solution)/shard_map/psum | solution.py:187
  280.6 2.4 convert_reduce_fusion.3
  289.1 6.5 all-reduce.2
  298.0 104.5 %while.43 = (s32[]{:T(128)}, f32[3,512,64]{1,2,0:T(8,128)S(1)}, f32[2,2048,384]{2,1,0:T(8,128)}, s32[512]{0:T(512)S(1)}, s32[2]{0:T(128)}, /*index=5*/s32[6,1]{0...) while((s32[]{:T(128)}, f32[3,512,64]{1,2,0:T(8,128)S(1)}, ...), condition=%wide.region_30.31_spmd.clone.clone.clone, body=%wide.region_27.30_spmd.clone.clone.clone.sunk | while | flops 2108366976 | bytes 175255120 | solution.py:274
  304.1 4.1 compare_and_fusion.13
  309.0 12.4 %fusion.216 = f32[3,512,2048]{1,2,0:T(8,128)S(1)} fusion(f32[3,512]{1,0:T(4,128)S(1)} %copy-done.86, f32[512,2048]{0,1:T(8,128)S(1)} %get-tuple-element.1766, pred[3,2048]{1,0:T(4,128)(4,1)S(1)} %broadcast_compare_fusion.46, pred[3,512]{1,0:T(4,128)(4,1)S(1)} %broadcast_compare_fusion.47, pred[512,2048]{0,1:T(8,128)(4,1)S(1)} %get-tuple-element.1771, ...), kind=kOutput, calls=%fused_computation.139.clone.1 | convolution fusion | flops 468713472 | bytes 22003716 | tf_op jit(solution)/shard_map/while/body/eval_jaxpr/hqd,khd->hqk/dot_general | solution.py:227
  321.4 5.1 fusion.217
  327.9 4.4 convolution_add_fusion.5
  332.3 6.7 fusion.218
  339.1 2.0 convolution_multiply_fusion.2
  343.0 3.5 copy.112
  346.5 3.7 constant_dynamic-update-slice_fusion.2
  356.4 4.1 compare_and_fusion.13
  361.2 12.4 %fusion.216 = f32[3,512,2048]{1,2,0:T(8,128)S(1)} fusion(f32[3,512]{1,0:T(4,128)S(1)} %copy-done.86, f32[512,2048]{0,1:T(8,128)S(1)} %get-tuple-element.1766, pred[3,2048]{1,0:T(4,128)(4,1)S(1)} %broadcast_compare_fusion.46, pred[3,512]{1,0:T(4,128)(4,1)S(1)} %broadcast_compare_fusion.47, pred[512,2048]{0,1:T(8,128)(4,1)S(1)} %get-tuple-element.1771, ...), kind=kOutput, calls=%fused_computation.139.clone.1 | convolution fusion | flops 468713472 | bytes 22003716 | tf_op jit(solution)/shard_map/while/body/eval_jaxpr/hqd,khd->hqk/dot_general | solution.py:227
  373.7 5.1 fusion.217
  380.1 4.4 convolution_add_fusion.5
  384.5 6.7 fusion.218
  395.2 3.5 copy.112
  398.7 3.8 constant_dynamic-update-slice_fusion.2
  402.8 2.1 multiply_convert_fusion
  406.6 2.2 fusion.144
  408.9 2.3 fusion.131
  413.6 2.5 fusion.142
  417.4 103.4 %reduce-scatter.8.cloned.1.call-done = f32[512,384]{1,0:T(8,128)} async-done(((f32[4096,384]{1,0:T(8,128)}), f32[512,384]{1,0:T(8,128)}) %reduce-scatter.8.cloned.1.call-update) | async-done | bytes 786448 | tf_op jit(solution)/shard_map/reduce_scatter | solution.py:276
  525.1 2.3 fusion.115
  531.6 14.2 %reduce-scatter.6.cloned.1.call-done = bf16[512,192]{0,1:T(8,128)(2,1)} async-done(((bf16[512,768]{0,1:T(8,128)(2,1)}), bf16[512,192]{0,1:T(8,128)(2,1)}) %reduce-scatter.6.cloned.1.call-update) | async-done | bytes 196624 | tf_op jit(solution)/shard_map/reduce_scatter | solution.py:170
  549.4 33.4 %all-reduce.10.cloned.1.call-done = bf16[512,768]{0,1:T(8,128)(2,1)} async-done(((bf16[512,768]{0,1:T(8,128)(2,1)}), bf16[512,768]{0,1:T(8,128)(2,1)}) %all-reduce.10.cloned.1.call-update) | async-done | bytes 786448 | tf_op jit(solution)/shard_map/psum | solution.py:291
  582.8 2.5 fusion.103
  585.3 40.1 %all-reduce = (f32[768]{0:T(1024)}, f32[768]{0:T(1024)}, f32[192]{0:T(256)}, f32[192]{0:T(256)}, f32[192]{0:T(256)}, /*index=5*/f32[192]{0:T(256)}, f32[768]{0:T...) all-reduce(f32[768]{0:T(1024)} %get-tuple-element.1251, ...), channel_id=1, replica_groups=mesh['seq'=8,'head'=4] {'seq'}, use_global_device_ids=true, to_apply=%region_36.37 | all-reduce | flops 6144 | bytes 49152 | tf_op jit(solution)/shard_map/psum | solution.py:296
  628.6 198.8 %all-reduce.12.cloned.1.call-done = (f32[768,192]{0,1:T(8,128)}, f32[768,192]{0,1:T(8,128)}, f32[768,192]{0,1:T(8,128)}, f32[192,768]{1,0:T(8,128)}, f32[768,768]{1,0:T(8,128)}, /*index=5*/f32[768,768]{1,0:T(8,128)}) async-done(((f32[768,192]{0,1:T(8,128)}, f32[768,192]{0,1:T(8,128)}, f32[768,192]{0,1:T(8,128)}, f32[192,768]{1,0:T(8,128)}, f32[768,768]{1,0:T(8,128)}, /*index=5*/f32[768,768]{1,0:T(8,128)}), ...) | async-done | bytes 7077904 | tf_op jit(solution)/shard_map/psum | solution.py:296
  827.4 2.0 copy.143
  (429 shorter events, 86.9 us)
Async XLA Ops:
  7.2 229.8 %copy-start = (bf16[768,768]{1,0:T(8,128)(2,1)S(1)}, bf16[768,768]{1,0:T(8,128)(2,1)}, u32[]{:S(2)}) copy-start(bf16[768,768]{1,0:T(8,128)(2,1)} %param.40) | copy-start | bytes 3538948
  7.2 11.5 %copy-start.87 = (f32[768]{0:T(1024)S(1)}, f32[768]{0:T(1024)}, u32[]{:S(2)}) copy-start(f32[768]{0:T(1024)} %param.26) | copy-start | bytes 9220
  7.2 11.5 %copy-start.70 = (f32[768]{0:T(1024)S(1)}, f32[768]{0:T(1024)}, u32[]{:S(2)}) copy-start(f32[768]{0:T(1024)} %param.25) | copy-start | bytes 9220
  7.2 59.4 %all-gather.3.cloned.1.call-start = ((), (), s32[]{:S(2)}) async-start(), calls=%async_computation.3 | async-start | bytes 1769472 | tf_op jit(solution)/shard_map/all_gather | solution.py:136
  20.3 92.5 %all-gather.5.cloned.1.call-start = ((), (), s32[]{:S(2)}) async-start(), calls=%async_computation.4 | async-start | bytes 1769472 | tf_op jit(solution)/shard_map/all_gather | solution.py:137
  21.4 204.1 %reduce-scatter.4.cloned.1.call-start = ((), (), s32[]{:S(2)}) async-start(), calls=%async_computation.5 | async-start | bytes 983040 | tf_op jit(solution)/shard_map/reduce_scatter | solution.py:156
  124.5 12.8 %copy-start.2 = (f32[512,2048]{0,1:T(8,128)}, f32[512,2048]{0,1:T(8,128)S(1)}, u32[]{:S(2)}) copy-start(f32[512,2048]{0,1:T(8,128)S(1)} %get-tuple-element.1711) | copy-start | bytes 12582916 | tf_op jit(solution)/shard_map/while
  124.5 12.8 %copy-start.3 = (pred[512,2048]{0,1:T(8,128)(4,1)}, pred[512,2048]{0,1:T(8,128)(4,1)S(1)}, u32[]{:S(2)}) copy-start(pred[512,2048]{0,1:T(8,128)(4,1)S(1)} %get-tuple-element.1720) | copy-start | bytes 3145732 | tf_op jit(solution)/shard_map/while
  124.5 12.8 %copy-start.4 = (pred[512,2048]{0,1:T(8,128)(4,1)}, pred[512,2048]{0,1:T(8,128)(4,1)S(1)}, u32[]{:S(2)}) copy-start(pred[512,2048]{0,1:T(8,128)(4,1)S(1)} %get-tuple-element.1716) | copy-start | bytes 3145732 | tf_op jit(solution)/shard_map/while
  125.1 12.3 %copy-start.55 = (pred[3,512]{1,0:T(4,128)(4,1)}, pred[3,512]{1,0:T(4,128)(4,1)S(1)}, u32[]{:S(2)}) copy-start(pred[3,512]{1,0:T(4,128)(4,1)S(1)} %broadcast_compare_fusion.43) | copy-start | bytes 4612 | tf_op jit(solution)/shard_map/while
  125.2 12.1 %copy-start.56 = (pred[3,512]{1,0:T(4,128)(4,1)}, pred[3,512]{1,0:T(4,128)(4,1)S(1)}, u32[]{:S(2)}) copy-start(pred[3,512]{1,0:T(4,128)(4,1)S(1)} %broadcast_compare_fusion.45) | copy-start | bytes 4612 | tf_op jit(solution)/shard_map/while
  137.4 16.7 %copy-start.43 = (f32[3,512]{1,0:T(4,128)S(1)}, f32[3,512]{1,0:T(4,128)}, u32[]{:S(2)}) copy-start(f32[3,512]{1,0:T(4,128)} %get-tuple-element.1804) | copy-start | bytes 18436 | tf_op jit(solution)/shard_map/while
  137.4 16.8 %copy-start.5 = (bf16[2,2048,3,64]{1,3,2,0:T(8,128)(2,1)S(1)}, bf16[2,2048,3,64]{1,3,2,0:T(8,128)(2,1)}, u32[]{:S(2)}) copy-start(bf16[2,2048,3,64]{1,3,2,0:T(8,128)(2,1)} %get-tuple-element.1834) | copy-start | bytes 4718596 | tf_op jit(solution)/shard_map/while
  137.4 16.8 %copy-start.17 = (f32[3,512,64]{1,2,0:T(8,128)S(1)}, f32[3,512,64]{1,2,0:T(8,128)}, u32[]{:S(2)}) copy-start(f32[3,512,64]{1,2,0:T(8,128)} %get-tuple-element.1805) | copy-start | bytes 1179652 | tf_op jit(solution)/shard_map/while
  163.4 12.8 %copy-start.2 = (f32[512,2048]{0,1:T(8,128)}, f32[512,2048]{0,1:T(8,128)S(1)}, u32[]{:S(2)}) copy-start(f32[512,2048]{0,1:T(8,128)S(1)} %get-tuple-element.1711) | copy-start | bytes 12582916 | tf_op jit(solution)/shard_map/while
  163.4 12.8 %copy-start.3 = (pred[512,2048]{0,1:T(8,128)(4,1)}, pred[512,2048]{0,1:T(8,128)(4,1)S(1)}, u32[]{:S(2)}) copy-start(pred[512,2048]{0,1:T(8,128)(4,1)S(1)} %get-tuple-element.1720) | copy-start | bytes 3145732 | tf_op jit(solution)/shard_map/while
  163.4 12.8 %copy-start.4 = (pred[512,2048]{0,1:T(8,128)(4,1)}, pred[512,2048]{0,1:T(8,128)(4,1)S(1)}, u32[]{:S(2)}) copy-start(pred[512,2048]{0,1:T(8,128)(4,1)S(1)} %get-tuple-element.1716) | copy-start | bytes 3145732 | tf_op jit(solution)/shard_map/while
  164.0 12.3 %copy-start.55 = (pred[3,512]{1,0:T(4,128)(4,1)}, pred[3,512]{1,0:T(4,128)(4,1)S(1)}, u32[]{:S(2)}) copy-start(pred[3,512]{1,0:T(4,128)(4,1)S(1)} %broadcast_compare_fusion.43) | copy-start | bytes 4612 | tf_op jit(solution)/shard_map/while
  164.1 12.1 %copy-start.56 = (pred[3,512]{1,0:T(4,128)(4,1)}, pred[3,512]{1,0:T(4,128)(4,1)S(1)}, u32[]{:S(2)}) copy-start(pred[3,512]{1,0:T(4,128)(4,1)S(1)} %broadcast_compare_fusion.45) | copy-start | bytes 4612 | tf_op jit(solution)/shard_map/while
  176.3 16.7 %copy-start.43 = (f32[3,512]{1,0:T(4,128)S(1)}, f32[3,512]{1,0:T(4,128)}, u32[]{:S(2)}) copy-start(f32[3,512]{1,0:T(4,128)} %get-tuple-element.1804) | copy-start | bytes 18436 | tf_op jit(solution)/shard_map/while
  176.3 16.8 %copy-start.5 = (bf16[2,2048,3,64]{1,3,2,0:T(8,128)(2,1)S(1)}, bf16[2,2048,3,64]{1,3,2,0:T(8,128)(2,1)}, u32[]{:S(2)}) copy-start(bf16[2,2048,3,64]{1,3,2,0:T(8,128)(2,1)} %get-tuple-element.1834) | copy-start | bytes 4718596 | tf_op jit(solution)/shard_map/while
  176.3 16.8 %copy-start.17 = (f32[3,512,64]{1,2,0:T(8,128)S(1)}, f32[3,512,64]{1,2,0:T(8,128)}, u32[]{:S(2)}) copy-start(f32[3,512,64]{1,2,0:T(8,128)} %get-tuple-element.1805) | copy-start | bytes 1179652 | tf_op jit(solution)/shard_map/while
  202.5 11.1 %copy-start.76 = (f32[512]{0:T(512)}, f32[512]{0:T(512)S(1)}, u32[]{:S(2)}) copy-start(f32[512]{0:T(512)S(1)} %get-tuple-element.1435) | copy-start | bytes 6148
  202.5 11.1 %copy-start.78 = (f32[512]{0:T(512)}, f32[512]{0:T(512)S(1)}, u32[]{:S(2)}) copy-start(f32[512]{0:T(512)S(1)} %get-tuple-element.1436) | copy-start | bytes 6148
  202.6 10.9 %copy-start.27 = (f32[512,192]{0,1:T(8,128)}, f32[512,192]{0,1:T(8,128)S(1)}, u32[]{:S(2)}) copy-start(f32[512,192]{0,1:T(8,128)S(1)} %fusion.112) | copy-start | bytes 1179652
  202.6 22.9 %copy-start.32 = (bf16[512,192]{0,1:T(8,128)(2,1)S(1)}, bf16[512,192]{0,1:T(8,128)(2,1)}, u32[]{:S(2)}) copy-start(bf16[512,192]{0,1:T(8,128)(2,1)} %param.24) | copy-start | bytes 589828
  204.0 76.6 %all-reduce.8.cloned.1.call-start = ((), (), s32[]{:S(2)}) async-start(), calls=%async_computation.7 | async-start | bytes 1572864 | tf_op jit(solution)/shard_map/psum | solution.py:187
  204.9 30.6 %copy-start.85 = (f32[192]{0:T(256)}, f32[192]{0:T(256)S(1)}, u32[]{:S(2)}) copy-start(f32[192]{0:T(256)S(1)} %dynamic_slice.65) | copy-start | bytes 2308
  213.5 23.4 %copy-start.23 = (bf16[512,768]{0,1:T(8,128)(2,1)}, bf16[512,768]{0,1:T(8,128)(2,1)S(1)}, u32[]{:S(2)}) copy-start(bf16[512,768]{0,1:T(8,128)(2,1)S(1)} %all_gather.21) | copy-start | bytes 2359300
  213.5 22.2 %copy-start.67 = (f32[768]{0:T(1024)S(1)}, f32[768]{0:T(1024)}, u32[]{:S(2)}) copy-start(f32[768]{0:T(1024)} %param.36) | copy-start | bytes 9220
  213.6 22.2 %copy-start.93 = (f32[768]{0:T(1024)S(1)}, f32[768]{0:T(1024)}, u32[]{:S(2)}) copy-start(f32[768]{0:T(1024)} %param.39) | copy-start | bytes 9220
  213.6 22.2 %copy-start.94 = (f32[768]{0:T(1024)S(1)}, f32[768]{0:T(1024)}, u32[]{:S(2)}) copy-start(f32[768]{0:T(1024)} %param.37) | copy-start | bytes 9220
  235.3 49.3 %copy-start.9 = (bf16[512,768]{0,1:T(8,128)(2,1)}, bf16[512,768]{0,1:T(8,128)(2,1)S(1)}, u32[]{:S(2)}) copy-start(bf16[512,768]{0,1:T(8,128)(2,1)S(1)} %all_gather.20) | copy-start | bytes 2359300
  235.5 49.1 %copy-start.65 = (f32[512]{0:T(512)}, f32[512]{0:T(512)S(1)}, u32[]{:S(2)}) copy-start(f32[512]{0:T(512)S(1)} %broadcast_multiply_fusion.1) | copy-start | bytes 6148
  235.8 48.8 %copy-start.74 = (f32[512]{0:T(512)}, f32[512]{0:T(512)S(1)}, u32[]{:S(2)}) copy-start(f32[512]{0:T(512)S(1)} %fusion.123) | copy-start | bytes 6148
  243.7 36.9 %copy-start.68 = (f32[768]{0:T(1024)S(1)}, f32[768]{0:T(1024)}, u32[]{:S(2)}) copy-start(f32[768]{0:T(1024)} %param.36) | copy-start | bytes 9220
  245.5 275.3 %reduce-scatter.8.cloned.1.call-start = ((), (), s32[]{:S(2)}) async-start(), calls=%async_computation.8 | async-start | bytes 7077888 | tf_op jit(solution)/shard_map/reduce_scatter | solution.py:276
  287.5 10.5 %copy-start.6 = (bf16[2,2048,3,64]{1,3,2,0:T(8,128)(2,1)S(1)}, bf16[2,2048,3,64]{1,3,2,0:T(8,128)(2,1)}, u32[]{:S(2)}) copy-start(bf16[2,2048,3,64]{1,3,2,0:T(8,128)(2,1)} %get-tuple-element.1936) | copy-start | bytes 4718596
  327.9 11.2 %slice-start = ((s8[6291456]{0:T(1024)(128)(4,1)}), s8[4194304]{0:T(1024)(128)(4,1)S(1)}, s32[]{:S(2)}) async-start(s8[6291456]{0:T(1024)(128)(4,1)} %bitcast.169), calls=%async_computation.11 | async-start | bytes 8388608 | tf_op jit(solution)/shard_map/while
  380.1 11.2 %slice-start = ((s8[6291456]{0:T(1024)(128)(4,1)}), s8[4194304]{0:T(1024)(128)(4,1)S(1)}, s32[]{:S(2)}) async-start(s8[6291456]{0:T(1024)(128)(4,1)} %bitcast.169), calls=%async_computation.11 | async-start | bytes 8388608 | tf_op jit(solution)/shard_map/while
  402.5 143.2 %reduce-scatter.6.cloned.1.call-start = ((), (), s32[]{:S(2)}) async-start(), calls=%async_computation.6 | async-start | bytes 983040 | tf_op jit(solution)/shard_map/reduce_scatter | solution.py:170
  411.2 171.6 %all-reduce.10.cloned.1.call-start = ((), (), s32[]{:S(2)}) async-start(), calls=%async_computation.9 | async-start | bytes 1572864 | tf_op jit(solution)/shard_map/psum | solution.py:291
  525.1 302.3 %all-reduce.12.cloned.1.call-start = ((), (), s32[]{:S(2)}) async-start(), calls=%async_computation.10 | async-start | bytes 14155776 | tf_op jit(solution)/shard_map/psum | solution.py:296
  528.8 54.0 %copy-start.64 = (f32[512]{0:T(512)S(1)}, f32[512]{0:T(512)}, u32[]{:S(2)}) copy-start(f32[512]{0:T(512)} %copy-done.63) | copy-start | bytes 6148
  528.8 54.0 %copy-start.71 = (f32[768]{0:T(1024)S(1)}, f32[768]{0:T(1024)}, u32[]{:S(2)}) copy-start(f32[768]{0:T(1024)} %param.25) | copy-start | bytes 9220
  528.8 54.0 %copy-start.73 = (f32[512]{0:T(512)S(1)}, f32[512]{0:T(512)}, u32[]{:S(2)}) copy-start(f32[512]{0:T(512)} %copy-done.72) | copy-start | bytes 6148
  528.8 54.0 %copy-start.12 = (bf16[512,768]{0,1:T(8,128)(2,1)S(1)}, bf16[512,768]{0,1:T(8,128)(2,1)}, u32[]{:S(2)}) copy-start(bf16[512,768]{0,1:T(8,128)(2,1)} %copy-done.11) | copy-start | bytes 2359300
  528.8 96.6 %copy-start.81 = (f32[512]{0:T(512)S(1)}, f32[512]{0:T(512)}, u32[]{:S(2)}) copy-start(f32[512]{0:T(512)} %copy-done.80) | copy-start | bytes 6148
  (87 other events, 307.0 us)
Sparse Core Ops, SparseCore 0:
  20.4 46.1 all-gather.2
  69.2 43.4 all-gather.4
  204.2 21.3 reduce-scatter.3
  245.6 34.9 all-reduce.7
  402.6 118.0 reduce-scatter.7
  523.3 22.3 reduce-scatter.5
  548.1 34.6 all-reduce.9
  589.6 237.7 all-reduce.11
where the time goes:
time: 852 us; the launch traced here: 843 us
  waiting for transfers between devices  482 us (57%)
  matrix products  120 us (14%)
  other arithmetic  95.7 us (11%)
  blocking collectives  80.4 us (9%)
  local copies, waits for them, and re-layouts  48.5 us (6%)
  between operations  15.1 us (2%)
    psum x1, waiting for transfers between devices, shards(): lax.psum((grad_ln1_gain, grad_ln1_bias, grad_w_query, grad_b_query, grad_...  199 us
    reduce_scatter x1, waiting for transfers between devices, shards(): lax.psum_scatter(key_terms, 'seq', scatter_dimension=0, tiled=True)  103 us
    all_gather x1, waiting for transfers between devices, shards(): lax.all_gather(key_rows, 'seq', axis=0, tiled=True)  43.9 us
    all_gather x1, waiting for transfers between devices, shards(): lax.all_gather(values, 'seq', axis=0, tiled=True)  41.5 us
    psum x1, blocking collectives, shards(): lax.psum((grad_ln1_gain, grad_ln1_bias, grad_w_query, grad_b_query, grad_...  40.1 us
    psum x1, waiting for transfers between devices, shards(): lax.psum(jnp.dot(grad_inner, w_up.T, preferred_element_type=jnp.float32)....  34.5 us
    psum x1, waiting for transfers between devices, shards(): lax.psum(grad_normed.astype(jnp.bfloat16), 'head').astype(jnp.float32)  33.4 us
    reduce_sum x2, other arithmetic, advance(): totals = totals * factor + jnp.sum(weights, axis=-1)  33.3 us
  transfers between devices with their start and end apart: 8, of which 8 were waited for; matrix products, arithmetic and copies ran while one was open for 5% of the time, Pallas kernels for 0%

commit v1 on v0

--- a/solution.py
+++ b/solution.py
@@ -288,7 +288,9 @@
         + jnp.dot(grad_keys, w_key.T, preferred_element_type=jnp.float32)
         + jnp.dot(grad_values, w_value.T, preferred_element_type=jnp.float32)
     )
-    grad_normed = lax.psum(grad_normed.astype(jnp.bfloat16), "head").astype(jnp.float32)
+    grad_normed = jnp.sum(lax.all_gather(grad_normed.astype(jnp.bfloat16), "head"), axis=0).astype(
+        jnp.float32
+    )
     unused, input_back = jax.vjp(layer_norm, input_whole, ln1_gain, ln1_bias)
     grad_in_norm, grad_ln1_gain, grad_ln1_bias = input_back(grad_normed)
     grad_input_whole = grad_middle + grad_in_norm

time: 852 us -> 846 us (level)
  waiting for transfers between devices: 482 us -> 472 us
    psum x1 -> x0, waiting for transfers between devices: 33.4 us -> none  [shards(): lax.psum(grad_normed.astype(jnp.bfloat16), 'head').astype(jnp.float32)]
    all_gather x0 -> x1, waiting for transfers between devices: none -> 27.6 us  [shards(): lax.all_gather(grad_normed.astype(jnp.bfloat16), 'head')]
    unnamed x158 -> x178, local copies, waits for them, and re-layouts: 15.4 us -> 18.8 us
where the time goes in v1:
time: 846 us; the launch traced here: 836 us
  waiting for transfers between devices  472 us (56%)
  matrix products  117 us (14%)
  other arithmetic  97.2 us (11%)
  blocking collectives  80.9 us (10%)
  local copies, waits for them, and re-layouts  53 us (6%)
  between operations  15.2 us (2%)
    psum x1, waiting for transfers between devices, shards(): lax.psum((grad_ln1_gain, grad_ln1_bias, grad_w_query, grad_b_query, grad_...  192 us
    reduce_scatter x1, waiting for transfers between devices, shards(): lax.psum_scatter(key_terms, 'seq', scatter_dimension=0, tiled=True)  110 us
    all_gather x1, waiting for transfers between devices, shards(): lax.all_gather(key_rows, 'seq', axis=0, tiled=True)  43.9 us
    all_gather x1, waiting for transfers between devices, shards(): lax.all_gather(values, 'seq', axis=0, tiled=True)  41.5 us
    psum x1, blocking collectives, shards(): lax.psum((grad_ln1_gain, grad_ln1_bias, grad_w_query, grad_b_query, grad_...  40.6 us
    psum x1, waiting for transfers between devices, shards(): lax.psum(jnp.dot(grad_inner, w_up.T, preferred_element_type=jnp.float32)....  34.5 us
    reduce_sum x2, other arithmetic, advance(): totals = totals * factor + jnp.sum(weights, axis=-1)  33.3 us
    all_gather x1, waiting for transfers between devices, shards(): lax.all_gather(grad_normed.astype(jnp.bfloat16), 'head')  27.6 us
  transfers between devices with their start and end apart: 8, of which 8 were waited for; matrix products, arithmetic and copies ran while one was open for 5% of the time, Pallas kernels for 0%

profile of v1, /device:TPU:0, one launch (start us, length us, event | category | flops | bytes accessed | tf_op | source)
XLA Modules:
  0.0 836.4 jit_solution(17438088587250301548)
XLA Ops:
  7.3 10.4 %all_gather.23 = bf16[512,768]{0,1:T(8,128)(2,1)S(1)} all-gather(bf16[512,192]{0,1:T(8,128)(2,1)} %param.24), channel_id=1, replica_groups=mesh['seq'=8,'head'=4] {'head'}, dimensions={1}, use_global_device_ids=true | all-gather | bytes 983040 | tf_op jit(solution)/shard_map/all_gather | solution.py:118
  22.8 43.9 %all-gather.5.cloned.1.call-done = bf16[4096,192]{0,1:T(8,128)(2,1)} async-done(((bf16[512,192]{0,1:T(8,128)(2,1)}), bf16[4096,192]{0,1:T(8,128)(2,1)}) %all-gather.5.cloned.1.call-update) | async-done | bytes 1572880 | tf_op jit(solution)/shard_map/all_gather | solution.py:136
  66.7 2.9 reshape.2798
  71.3 41.5 %all-gather.7.cloned.1.call-done = bf16[4096,192]{0,1:T(8,128)(2,1)} async-done(((bf16[512,192]{0,1:T(8,128)(2,1)}), bf16[4096,192]{0,1:T(8,128)(2,1)}) %all-gather.7.cloned.1.call-update) | async-done | bytes 1572880 | tf_op jit(solution)/shard_map/all_gather | solution.py:137
  112.8 2.9 reshape.2800
  117.4 77.7 %while.42 = (s32[]{:T(128)}, f32[3,512]{1,0:T(4,128)S(1)}, f32[3,512]{1,0:T(4,128)}, f32[3,512,64]{1,2,0:T(8,128)}, s32[512]{0:T(512)S(1)}, /*index=5*/s32[2]{0:...) while((s32[]{:T(128)}, f32[3,512]{1,0:T(4,128)S(1)}, ...), condition=%wide.region_10.11_spmd.clone.clone.clone, body=%wide.region_5.10_spmd.clone.clone.clone.sunk | while | flops 955956864 | bytes 106965376 | solution.py:81
  120.4 4.1 compare_and_fusion.12
  125.3 12.1 %fusion.202 = (f32[3,512]{1,0:T(4,128)S(1)}, f32[3,2048,512]{2,1,0:T(8,128)}) fusion(f32[512,2048]{0,1:T(8,128)S(1)} %get-tuple-element.1745, pred[3,2048]{1,0:T(4,128)(4,1)S(1)} %broadcast_compare_fusion.38, pred[3,512]{1,0:T(4,128)(4,1)S(1)} %broadcast_compare_fusion.39, pred[512,2048]{0,1:T(8,128)(4,1)S(1)} %get-tuple-element.1750, ...), kind=kOutput, calls=%fused_computation.7.clone.1 | convolution fusion | flops 465566208 | bytes 22001668 | tf_op jit(solution)/shard_map/while/body/eval_jaxpr/hqd,khd->hqk/dot_general | solution.py:65
  137.4 16.7 %fusion.203 = (f32[3,512]{1,0:T(4,128)S(1)}, bf16[3,512,2048]{1,2,0:T(8,128)(2,1)S(1)}) fusion(f32[3,512]{1,0:T(4,128)S(1)} %select_maximum_fusion.2, f32[3,2048,512]{2,1,0:T(8,128)} %get-tuple-element.1764, pred[3,2048]{1,0:T(4,128)(4,1)S(1)} %broadcast_compare_fusion.38, pred[3,512]{1,0:T(4,128)(4,1)S(1)} %broadcast_compare_fusion.39, ...), kind=kLoop, calls=%fused_computation.388.clone.1 | loop fusion | flops 72350208 | bytes 27305984 | tf_op jit(solution)/shard_map/while/body/eval_jaxpr/reduce_sum | solution.py:72
  159.3 4.1 compare_and_fusion.12
  164.2 12.1 %fusion.202 = (f32[3,512]{1,0:T(4,128)S(1)}, f32[3,2048,512]{2,1,0:T(8,128)}) fusion(f32[512,2048]{0,1:T(8,128)S(1)} %get-tuple-element.1745, pred[3,2048]{1,0:T(4,128)(4,1)S(1)} %broadcast_compare_fusion.38, pred[3,512]{1,0:T(4,128)(4,1)S(1)} %broadcast_compare_fusion.39, pred[512,2048]{0,1:T(8,128)(4,1)S(1)} %get-tuple-element.1750, ...), kind=kOutput, calls=%fused_computation.7.clone.1 | convolution fusion | flops 465566208 | bytes 22001668 | tf_op jit(solution)/shard_map/while/body/eval_jaxpr/hqd,khd->hqk/dot_general | solution.py:65
  176.3 16.7 %fusion.203 = (f32[3,512]{1,0:T(4,128)S(1)}, bf16[3,512,2048]{1,2,0:T(8,128)(2,1)S(1)}) fusion(f32[3,512]{1,0:T(4,128)S(1)} %select_maximum_fusion.2, f32[3,2048,512]{2,1,0:T(8,128)} %get-tuple-element.1764, pred[3,2048]{1,0:T(4,128)(4,1)S(1)} %broadcast_compare_fusion.38, pred[3,512]{1,0:T(4,128)(4,1)S(1)} %broadcast_compare_fusion.39, ...), kind=kLoop, calls=%fused_computation.388.clone.1 | loop fusion | flops 72350208 | bytes 27305984 | tf_op jit(solution)/shard_map/while/body/eval_jaxpr/reduce_sum | solution.py:72
  196.4 6.0 all-reduce.3
  204.9 8.7 %all_gather.27 = bf16[512,768]{0,1:T(8,128)(2,1)S(1)} all-gather(bf16[512,192]{0,1:T(8,128)(2,1)} %param.42), channel_id=1, replica_groups=mesh['seq'=8,'head'=4] {'head'}, dimensions={1}, use_global_device_ids=true | all-gather | bytes 983040 | tf_op jit(solution)/shard_map/all_gather | solution.py:178
  213.6 11.9 %reduce-scatter.4.cloned.1.call-done = bf16[512,192]{0,1:T(8,128)(2,1)} async-done(((bf16[512,768]{0,1:T(8,128)(2,1)}), bf16[512,192]{0,1:T(8,128)(2,1)}) %reduce-scatter.4.cloned.1.call-update) | async-done | bytes 196624 | tf_op jit(solution)/shard_map/reduce_scatter | solution.py:156
  226.7 8.7 %all_gather.26 = bf16[512,768]{0,1:T(8,128)(2,1)S(1)} all-gather(bf16[512,192]{0,1:T(8,128)(2,1)S(1)} %fusion.114), channel_id=1, replica_groups=mesh['seq'=8,'head'=4] {'head'}, dimensions={1}, use_global_device_ids=true | all-gather | bytes 983040 | tf_op jit(solution)/shard_map/all_gather | solution.py:164
  237.0 5.8 convert_reduce_fusion.7
  246.1 34.5 %all-reduce.7.cloned.1.call-done = bf16[512,768]{0,1:T(8,128)(2,1)} async-done(((bf16[512,768]{0,1:T(8,128)(2,1)}), bf16[512,768]{0,1:T(8,128)(2,1)}) %all-reduce.7.cloned.1.call-update) | async-done | bytes 786448 | tf_op jit(solution)/shard_map/psum | solution.py:187
  280.6 2.4 convert_reduce_fusion.3
  289.1 6.5 all-reduce.2
  298.0 104.7 %while.43 = (s32[]{:T(128)}, f32[3,512,64]{1,2,0:T(8,128)S(1)}, f32[2,2048,384]{2,1,0:T(8,128)}, s32[512]{0:T(512)S(1)}, s32[2]{0:T(128)}, /*index=5*/s32[6,1]{0...) while((s32[]{:T(128)}, f32[3,512,64]{1,2,0:T(8,128)S(1)}, ...), condition=%wide.region_30.31_spmd.clone.clone.clone, body=%wide.region_27.30_spmd.clone.clone.clone.sunk | while | flops 2108366976 | bytes 175255120 | solution.py:274
  304.2 4.1 compare_and_fusion.13
  309.1 12.4 %fusion.216 = f32[3,512,2048]{1,2,0:T(8,128)S(1)} fusion(f32[3,512]{1,0:T(4,128)S(1)} %copy-done.96, f32[512,2048]{0,1:T(8,128)S(1)} %get-tuple-element.1800, pred[3,2048]{1,0:T(4,128)(4,1)S(1)} %broadcast_compare_fusion.46, pred[3,512]{1,0:T(4,128)(4,1)S(1)} %broadcast_compare_fusion.47, pred[512,2048]{0,1:T(8,128)(4,1)S(1)} %get-tuple-element.1805, ...), kind=kOutput, calls=%fused_computation.139.clone.1 | convolution fusion | flops 468713472 | bytes 22003716 | tf_op jit(solution)/shard_map/while/body/eval_jaxpr/hqd,khd->hqk/dot_general | solution.py:227
  321.5 5.2 fusion.217
  328.0 4.4 convolution_add_fusion.5
  332.4 6.7 fusion.218
  339.2 2.0 convolution_multiply_fusion.2
  343.1 3.5 copy.112
  346.6 3.7 constant_dynamic-update-slice_fusion.2
  356.6 4.1 compare_and_fusion.13
  361.4 12.4 %fusion.216 = f32[3,512,2048]{1,2,0:T(8,128)S(1)} fusion(f32[3,512]{1,0:T(4,128)S(1)} %copy-done.96, f32[512,2048]{0,1:T(8,128)S(1)} %get-tuple-element.1800, pred[3,2048]{1,0:T(4,128)(4,1)S(1)} %broadcast_compare_fusion.46, pred[3,512]{1,0:T(4,128)(4,1)S(1)} %broadcast_compare_fusion.47, pred[512,2048]{0,1:T(8,128)(4,1)S(1)} %get-tuple-element.1805, ...), kind=kOutput, calls=%fused_computation.139.clone.1 | convolution fusion | flops 468713472 | bytes 22003716 | tf_op jit(solution)/shard_map/while/body/eval_jaxpr/hqd,khd->hqk/dot_general | solution.py:227
  373.9 5.2 fusion.217
  380.3 4.4 convolution_add_fusion.5
  384.8 6.7 fusion.218
  391.5 2.0 convolution_multiply_fusion.2
  395.4 3.5 copy.112
  399.0 3.8 constant_dynamic-update-slice_fusion.2
  411.0 110.1 %reduce-scatter.8.cloned.1.call-done = f32[512,384]{1,0:T(8,128)} async-done(((f32[4096,384]{1,0:T(8,128)}), f32[512,384]{1,0:T(8,128)}) %reduce-scatter.8.cloned.1.call-update) | async-done | bytes 786448 | tf_op jit(solution)/shard_map/reduce_scatter | solution.py:276
  524.6 2.2 fusion.144
  526.9 2.3 fusion.131
  536.3 9.7 %reduce-scatter.6.cloned.1.call-done = bf16[512,192]{0,1:T(8,128)(2,1)} async-done(((bf16[512,768]{0,1:T(8,128)(2,1)}), bf16[512,192]{0,1:T(8,128)(2,1)}) %reduce-scatter.6.cloned.1.call-update) | async-done | bytes 196624 | tf_op jit(solution)/shard_map/reduce_scatter | solution.py:170
  548.6 27.6 %all-gather.9.cloned.1.call-done = bf16[2048,768]{1,0:T(8,128)(2,1)} async-done(((bf16[512,768]{1,0:T(8,128)(2,1)}), bf16[2048,768]{1,0:T(8,128)(2,1)}) %all-gather.9.cloned.1.call-update) | async-done | bytes 3145744 | tf_op jit(solution)/shard_map/all_gather | solution.py:291
  576.2 3.5 reduce_sum.387
  579.7 2.4 copy.79
  582.1 2.5 fusion.103
  584.6 40.6 %all-reduce = (f32[768]{0:T(1024)}, f32[768]{0:T(1024)}, f32[192]{0:T(256)}, f32[192]{0:T(256)}, f32[192]{0:T(256)}, /*index=5*/f32[192]{0:T(256)}, f32[768]{0:T...) all-reduce(f32[768]{0:T(1024)} %get-tuple-element.1285, ...), channel_id=1, replica_groups=mesh['seq'=8,'head'=4] {'seq'}, use_global_device_ids=true, to_apply=%region_36.37 | all-reduce | flops 6144 | bytes 49152 | tf_op jit(solution)/shard_map/psum | solution.py:298
  628.5 192.4 %all-reduce.9.cloned.1.call-done = (f32[768,192]{0,1:T(8,128)}, f32[768,192]{0,1:T(8,128)}, f32[768,192]{0,1:T(8,128)}, f32[192,768]{1,0:T(8,128)}, f32[768,768]{1,0:T(8,128)}, /*index=5*/f32[768,768]{1,0:T(8,128)}) async-done(((f32[768,192]{0,1:T(8,128)}, f32[768,192]{0,1:T(8,128)}, f32[768,192]{0,1:T(8,128)}, f32[192,768]{1,0:T(8,128)}, f32[768,768]{1,0:T(8,128)}, /*index=5*/f32[768,768]{1,0:T(8,128)}), ...) | async-done | bytes 7077904 | tf_op jit(solution)/shard_map/psum | solution.py:298
  820.9 2.0 copy.142
  (451 shorter events, 88.6 us)
Async XLA Ops:
  7.2 229.8 %copy-start = (bf16[768,768]{1,0:T(8,128)(2,1)S(1)}, bf16[768,768]{1,0:T(8,128)(2,1)}, u32[]{:S(2)}) copy-start(bf16[768,768]{1,0:T(8,128)(2,1)} %param.40) | copy-start | bytes 3538948
  7.2 11.5 %copy-start.97 = (f32[768]{0:T(1024)S(1)}, f32[768]{0:T(1024)}, u32[]{:S(2)}) copy-start(f32[768]{0:T(1024)} %param.26) | copy-start | bytes 9220
  7.2 11.5 %copy-start.79 = (f32[768]{0:T(1024)S(1)}, f32[768]{0:T(1024)}, u32[]{:S(2)}) copy-start(f32[768]{0:T(1024)} %param.25) | copy-start | bytes 9220
  7.2 59.4 %all-gather.5.cloned.1.call-start = ((), (), s32[]{:S(2)}) async-start(), calls=%async_computation.3 | async-start | bytes 1769472 | tf_op jit(solution)/shard_map/all_gather | solution.py:136
  20.3 92.5 %all-gather.7.cloned.1.call-start = ((), (), s32[]{:S(2)}) async-start(), calls=%async_computation.4 | async-start | bytes 1769472 | tf_op jit(solution)/shard_map/all_gather | solution.py:137
  21.4 204.1 %reduce-scatter.4.cloned.1.call-start = ((), (), s32[]{:S(2)}) async-start(), calls=%async_computation.5 | async-start | bytes 983040 | tf_op jit(solution)/shard_map/reduce_scatter | solution.py:156
  124.6 12.8 %copy-start.2 = (f32[512,2048]{0,1:T(8,128)}, f32[512,2048]{0,1:T(8,128)S(1)}, u32[]{:S(2)}) copy-start(f32[512,2048]{0,1:T(8,128)S(1)} %get-tuple-element.1745) | copy-start | bytes 12582916 | tf_op jit(solution)/shard_map/while
  124.6 12.8 %copy-start.3 = (pred[512,2048]{0,1:T(8,128)(4,1)}, pred[512,2048]{0,1:T(8,128)(4,1)S(1)}, u32[]{:S(2)}) copy-start(pred[512,2048]{0,1:T(8,128)(4,1)S(1)} %get-tuple-element.1754) | copy-start | bytes 3145732 | tf_op jit(solution)/shard_map/while
  124.6 12.8 %copy-start.4 = (pred[512,2048]{0,1:T(8,128)(4,1)}, pred[512,2048]{0,1:T(8,128)(4,1)S(1)}, u32[]{:S(2)}) copy-start(pred[512,2048]{0,1:T(8,128)(4,1)S(1)} %get-tuple-element.1750) | copy-start | bytes 3145732 | tf_op jit(solution)/shard_map/while
  125.1 12.3 %copy-start.64 = (pred[3,512]{1,0:T(4,128)(4,1)}, pred[3,512]{1,0:T(4,128)(4,1)S(1)}, u32[]{:S(2)}) copy-start(pred[3,512]{1,0:T(4,128)(4,1)S(1)} %broadcast_compare_fusion.43) | copy-start | bytes 4612 | tf_op jit(solution)/shard_map/while
  125.3 12.1 %copy-start.65 = (pred[3,512]{1,0:T(4,128)(4,1)}, pred[3,512]{1,0:T(4,128)(4,1)S(1)}, u32[]{:S(2)}) copy-start(pred[3,512]{1,0:T(4,128)(4,1)S(1)} %broadcast_compare_fusion.45) | copy-start | bytes 4612 | tf_op jit(solution)/shard_map/while
  137.4 16.7 %copy-start.52 = (f32[3,512]{1,0:T(4,128)S(1)}, f32[3,512]{1,0:T(4,128)}, u32[]{:S(2)}) copy-start(f32[3,512]{1,0:T(4,128)} %get-tuple-element.1838) | copy-start | bytes 18436 | tf_op jit(solution)/shard_map/while
  137.4 16.8 %copy-start.5 = (bf16[2,2048,3,64]{1,3,2,0:T(8,128)(2,1)S(1)}, bf16[2,2048,3,64]{1,3,2,0:T(8,128)(2,1)}, u32[]{:S(2)}) copy-start(bf16[2,2048,3,64]{1,3,2,0:T(8,128)(2,1)} %get-tuple-element.1868) | copy-start | bytes 4718596 | tf_op jit(solution)/shard_map/while
  137.4 16.8 %copy-start.17 = (f32[3,512,64]{1,2,0:T(8,128)S(1)}, f32[3,512,64]{1,2,0:T(8,128)}, u32[]{:S(2)}) copy-start(f32[3,512,64]{1,2,0:T(8,128)} %get-tuple-element.1839) | copy-start | bytes 1179652 | tf_op jit(solution)/shard_map/while
  163.4 12.8 %copy-start.2 = (f32[512,2048]{0,1:T(8,128)}, f32[512,2048]{0,1:T(8,128)S(1)}, u32[]{:S(2)}) copy-start(f32[512,2048]{0,1:T(8,128)S(1)} %get-tuple-element.1745) | copy-start | bytes 12582916 | tf_op jit(solution)/shard_map/while
  163.4 12.8 %copy-start.3 = (pred[512,2048]{0,1:T(8,128)(4,1)}, pred[512,2048]{0,1:T(8,128)(4,1)S(1)}, u32[]{:S(2)}) copy-start(pred[512,2048]{0,1:T(8,128)(4,1)S(1)} %get-tuple-element.1754) | copy-start | bytes 3145732 | tf_op jit(solution)/shard_map/while
  163.4 12.8 %copy-start.4 = (pred[512,2048]{0,1:T(8,128)(4,1)}, pred[512,2048]{0,1:T(8,128)(4,1)S(1)}, u32[]{:S(2)}) copy-start(pred[512,2048]{0,1:T(8,128)(4,1)S(1)} %get-tuple-element.1750) | copy-start | bytes 3145732 | tf_op jit(solution)/shard_map/while
  164.0 12.3 %copy-start.64 = (pred[3,512]{1,0:T(4,128)(4,1)}, pred[3,512]{1,0:T(4,128)(4,1)S(1)}, u32[]{:S(2)}) copy-start(pred[3,512]{1,0:T(4,128)(4,1)S(1)} %broadcast_compare_fusion.43) | copy-start | bytes 4612 | tf_op jit(solution)/shard_map/while
  164.1 12.1 %copy-start.65 = (pred[3,512]{1,0:T(4,128)(4,1)}, pred[3,512]{1,0:T(4,128)(4,1)S(1)}, u32[]{:S(2)}) copy-start(pred[3,512]{1,0:T(4,128)(4,1)S(1)} %broadcast_compare_fusion.45) | copy-start | bytes 4612 | tf_op jit(solution)/shard_map/while
  176.3 16.7 %copy-start.52 = (f32[3,512]{1,0:T(4,128)S(1)}, f32[3,512]{1,0:T(4,128)}, u32[]{:S(2)}) copy-start(f32[3,512]{1,0:T(4,128)} %get-tuple-element.1838) | copy-start | bytes 18436 | tf_op jit(solution)/shard_map/while
  176.3 16.8 %copy-start.5 = (bf16[2,2048,3,64]{1,3,2,0:T(8,128)(2,1)S(1)}, bf16[2,2048,3,64]{1,3,2,0:T(8,128)(2,1)}, u32[]{:S(2)}) copy-start(bf16[2,2048,3,64]{1,3,2,0:T(8,128)(2,1)} %get-tuple-element.1868) | copy-start | bytes 4718596 | tf_op jit(solution)/shard_map/while
  176.3 16.8 %copy-start.17 = (f32[3,512,64]{1,2,0:T(8,128)S(1)}, f32[3,512,64]{1,2,0:T(8,128)}, u32[]{:S(2)}) copy-start(f32[3,512,64]{1,2,0:T(8,128)} %get-tuple-element.1839) | copy-start | bytes 1179652 | tf_op jit(solution)/shard_map/while
  202.5 11.0 %copy-start.85 = (f32[512]{0:T(512)}, f32[512]{0:T(512)S(1)}, u32[]{:S(2)}) copy-start(f32[512]{0:T(512)S(1)} %get-tuple-element.1469) | copy-start | bytes 6148
  202.5 11.0 %copy-start.87 = (f32[512]{0:T(512)}, f32[512]{0:T(512)S(1)}, u32[]{:S(2)}) copy-start(f32[512]{0:T(512)S(1)} %get-tuple-element.1470) | copy-start | bytes 6148
  202.6 10.9 %copy-start.27 = (f32[512,192]{0,1:T(8,128)}, f32[512,192]{0,1:T(8,128)S(1)}, u32[]{:S(2)}) copy-start(f32[512,192]{0,1:T(8,128)S(1)} %fusion.112) | copy-start | bytes 1179652
  202.6 22.9 %copy-start.34 = (bf16[512,192]{0,1:T(8,128)(2,1)S(1)}, bf16[512,192]{0,1:T(8,128)(2,1)}, u32[]{:S(2)}) copy-start(bf16[512,192]{0,1:T(8,128)(2,1)} %param.24) | copy-start | bytes 589828
  204.1 76.6 %all-reduce.7.cloned.1.call-start = ((), (), s32[]{:S(2)}) async-start(), calls=%async_computation.7 | async-start | bytes 1572864 | tf_op jit(solution)/shard_map/psum | solution.py:187
  204.9 30.6 %copy-start.94 = (f32[192]{0:T(256)}, f32[192]{0:T(256)S(1)}, u32[]{:S(2)}) copy-start(f32[192]{0:T(256)S(1)} %dynamic_slice.65) | copy-start | bytes 2308
  213.5 23.4 %copy-start.23 = (bf16[512,768]{0,1:T(8,128)(2,1)}, bf16[512,768]{0,1:T(8,128)(2,1)S(1)}, u32[]{:S(2)}) copy-start(bf16[512,768]{0,1:T(8,128)(2,1)S(1)} %all_gather.27) | copy-start | bytes 2359300
  213.5 22.2 %copy-start.76 = (f32[768]{0:T(1024)S(1)}, f32[768]{0:T(1024)}, u32[]{:S(2)}) copy-start(f32[768]{0:T(1024)} %param.36) | copy-start | bytes 9220
  213.6 22.2 %copy-start.103 = (f32[768]{0:T(1024)S(1)}, f32[768]{0:T(1024)}, u32[]{:S(2)}) copy-start(f32[768]{0:T(1024)} %param.39) | copy-start | bytes 9220
  213.6 22.2 %copy-start.104 = (f32[768]{0:T(1024)S(1)}, f32[768]{0:T(1024)}, u32[]{:S(2)}) copy-start(f32[768]{0:T(1024)} %param.37) | copy-start | bytes 9220
  235.3 49.2 %copy-start.9 = (bf16[512,768]{0,1:T(8,128)(2,1)}, bf16[512,768]{0,1:T(8,128)(2,1)S(1)}, u32[]{:S(2)}) copy-start(bf16[512,768]{0,1:T(8,128)(2,1)S(1)} %all_gather.26) | copy-start | bytes 2359300
  235.5 49.1 %copy-start.74 = (f32[512]{0:T(512)}, f32[512]{0:T(512)S(1)}, u32[]{:S(2)}) copy-start(f32[512]{0:T(512)S(1)} %broadcast_multiply_fusion.1) | copy-start | bytes 6148
  235.8 48.8 %copy-start.83 = (f32[512]{0:T(512)}, f32[512]{0:T(512)S(1)}, u32[]{:S(2)}) copy-start(f32[512]{0:T(512)S(1)} %fusion.123) | copy-start | bytes 6148
  243.7 36.9 %copy-start.77 = (f32[768]{0:T(1024)S(1)}, f32[768]{0:T(1024)}, u32[]{:S(2)}) copy-start(f32[768]{0:T(1024)} %param.36) | copy-start | bytes 9220
  245.4 275.6 %reduce-scatter.8.cloned.1.call-start = ((), (), s32[]{:S(2)}) async-start(), calls=%async_computation.8 | async-start | bytes 7077888 | tf_op jit(solution)/shard_map/reduce_scatter | solution.py:276
  328.0 11.2 %slice-start = ((s8[6291456]{0:T(1024)(128)(4,1)}), s8[4194304]{0:T(1024)(128)(4,1)S(1)}, s32[]{:S(2)}) async-start(s8[6291456]{0:T(1024)(128)(4,1)} %bitcast.170), calls=%async_computation.11 | async-start | bytes 8388608 | tf_op jit(solution)/shard_map/while
  380.3 11.2 %slice-start = ((s8[6291456]{0:T(1024)(128)(4,1)}), s8[4194304]{0:T(1024)(128)(4,1)S(1)}, s32[]{:S(2)}) async-start(s8[6291456]{0:T(1024)(128)(4,1)} %bitcast.170), calls=%async_computation.11 | async-start | bytes 8388608 | tf_op jit(solution)/shard_map/while
  402.8 143.3 %reduce-scatter.6.cloned.1.call-start = ((), (), s32[]{:S(2)}) async-start(), calls=%async_computation.6 | async-start | bytes 983040 | tf_op jit(solution)/shard_map/reduce_scatter | solution.py:170
  408.4 167.8 %all-gather.9.cloned.1.call-start = ((), (), s32[]{:S(2)}) async-start(), calls=%async_computation.9 | async-start | bytes 3932160 | tf_op jit(solution)/shard_map/all_gather | solution.py:291
  409.4 112.9 %copy-start.43 = (bf16[768,192]{0,1:T(8,128)(2,1)S(1)}, bf16[768,192]{0,1:T(8,128)(2,1)}, u32[]{:S(2)}) copy-start(bf16[768,192]{0,1:T(8,128)(2,1)} %param.29) | copy-start | bytes 884740
  411.0 112.1 %copy-start.41 = (bf16[768,192]{0,1:T(8,128)(2,1)S(1)}, bf16[768,192]{0,1:T(8,128)(2,1)}, u32[]{:S(2)}) copy-start(bf16[768,192]{0,1:T(8,128)(2,1)} %param.30) | copy-start | bytes 884740
  524.5 296.4 %all-reduce.9.cloned.1.call-start = ((), (), s32[]{:S(2)}) async-start(), calls=%async_computation.10 | async-start | bytes 14155776 | tf_op jit(solution)/shard_map/psum | solution.py:298
  534.9 11.2 %copy-start.35 = (bf16[512,192]{0,1:T(8,128)(2,1)S(1)}, bf16[512,192]{0,1:T(8,128)(2,1)}, u32[]{:S(2)}) copy-start(bf16[512,192]{0,1:T(8,128)(2,1)} %param.24) | copy-start | bytes 589828
  534.9 11.2 %copy-start.48 = (bf16[512,192]{0,1:T(8,128)(2,1)S(1)}, bf16[512,192]{0,1:T(8,128)(2,1)}, u32[]{:S(2)}) copy-start(bf16[512,192]{0,1:T(8,128)(2,1)} %reduce-scatter.4.cloned.1.call-done) | copy-start | bytes 589828
  534.9 11.2 %copy-start.95 = (f32[192]{0:T(256)S(1)}, f32[192]{0:T(256)}, u32[]{:S(2)}) copy-start(f32[192]{0:T(256)} %copy-done.94) | copy-start | bytes 2308
  579.7 45.6 %copy-start.90 = (f32[512]{0:T(512)S(1)}, f32[512]{0:T(512)}, u32[]{:S(2)}) copy-start(f32[512]{0:T(512)} %copy-done.89) | copy-start | bytes 6148
  (97 other events, 328.5 us)
Sparse Core Ops, SparseCore 0:
  20.4 46.1 all-gather.4
  69.3 43.4 all-gather.6
  204.2 21.3 reduce-scatter.3
  245.6 35.0 all-reduce.6
  402.9 118.1 reduce-scatter.7
  523.6 22.4 reduce-scatter.5
  547.6 28.5 all-gather.8
  583.0 237.8 all-reduce.8
